TPU v7x, 256 devices: a whole 4x4x8 slice. The times are simulated.
256 devices in a mesh: row: 32 (over y, z), col: 8 (over x, core).
Axes of the slice: x: 4, y: 4, z: 8, core: 2. Of those that a mesh axis runs over, the one named last changes fastest.
Arguments:
- trail_adjoint: float32 [24576, 24576], P('row', 'col'), may hold values from -3 to 3
- panel: float32 [24576, 256], P(('row', 'col')), may hold values from -0.0390625 to 0.0390625
- panel_adjoint: float32 [24576, 256], P(('row', 'col')), may hold values from -6 to 6
- diag_factor: float32 [256, 256], replicated, as said below
- diag_inverse: float32 [256, 256], replicated, as said below
- diag_adjoint: float32 [256, 256], replicated, may hold values from -6 to 6
Outputs:
- panel_grad: float32 [24576, 256], P(('row', 'col'))
- diag_grad: float32 [256, 256], replicated
Inputs may be any that keep to these rules, and one draw needn't show every extreme that they name: diag_factor is lower triangular with a diagonal between 1 and 2, and diag_inverse is its inverse. diag_factor is lower triangular with a diagonal between 1 and 2.
All inputs are finite; a program needn't handle non-finite values.
Results may differ from a plain program's by a relative error of at most 0.000057.
Values sent between devices are 32-bit elements; how exact they have to be, the bound alone decides.
A program may use at most 128 MiB of HBM per device.

v0:
```python
import jax
import jax.numpy as jnp
from jax import lax
from jax.sharding import PartitionSpec as P


def lower_half(matrix):
    return jnp.tril(matrix) - 0.5 * jnp.diag(jnp.diag(matrix))


def on_device(trail_adjoint, panel, panel_adjoint, diag_factor, diag_inverse, diag_adjoint):
    highest = lax.Precision.HIGHEST
    col_place = lax.axis_index("col")
    trail_width = trail_adjoint.shape[1]
    row_block = lax.all_gather(panel, "col", axis=0, tiled=True)
    full_panel = lax.all_gather(row_block, "row", axis=0, tiled=True)
    column_panel = lax.dynamic_slice_in_dim(full_panel, col_place * trail_width, trail_width, 0)
    image = lax.psum_scatter(
        jnp.dot(trail_adjoint, column_panel, precision=highest, preferred_element_type=jnp.float32),
        "col",
        scatter_dimension=0,
        tiled=True,
    )
    updated = panel_adjoint - 2.0 * image
    panel_grad = jnp.dot(
        updated, diag_inverse, precision=highest, preferred_element_type=jnp.float32
    )
    local_gram = jnp.dot(panel_grad.T, panel, precision=highest, preferred_element_type=jnp.float32)
    gram = lax.psum(local_gram, ("row", "col"))
    corner = diag_adjoint - gram
    inner = lower_half(
        jnp.dot(diag_factor.T, corner, precision=highest, preferred_element_type=jnp.float32)
    )
    left_part = jnp.dot(
        diag_inverse.T, inner, precision=highest, preferred_element_type=jnp.float32
    )
    diag_grad = lower_half(
        jnp.dot(left_part, diag_inverse, precision=highest, preferred_element_type=jnp.float32)
    )
    return (panel_grad, diag_grad)


def solution(mesh):
    in_specs = (P("row", "col"), P(("row", "col"), None), P(("row", "col"), None), P(), P(), P())
    out_specs = (P(("row", "col"), None), P())
    return jax.shard_map(
        on_device, mesh=mesh, in_specs=in_specs, out_specs=out_specs, check_vma=False
    )
```

profile of v0, /device:TPU:2, one launch (start us, length us, event | category | flops | bytes accessed | tf_op | source)
XLA Modules:
  0.0 522.4 jit_solution(10304371956958443014)
XLA Ops:
  7.2 0.0 copy-start
  7.2 0.0 copy-start.1
  7.2 0.0 copy-start.5
  7.2 0.0 copy-start.3
  7.2 0.0 copy-start.4
  7.2 0.0 all-gather.2.cloned.1.call-start
  7.3 14.9 %all_gather.6 = f32[768,256]{1,0:T(8,128)} all-gather(f32[96,256]{1,0:T(8,128)} %param.7), channel_id=1, replica_groups=mesh['row'=32,'col'=8] {'col'}, dimensions={0}, use_global_device_ids=true | all-gather | bytes 884736 | tf_op jit(solution)/shard_map/all_gather | solution.py:15
  22.1 0.0 all-gather.2.cloned.1.call-update
  22.2 0.0 reduce-scatter.2.cloned.1.call-start
  22.2 186.5 %all-gather.2.cloned.1.call-done = f32[24576,256]{1,0:T(8,128)} async-done(((f32[768,256]{1,0:T(8,128)}), f32[24576,256]{1,0:T(8,128)}) %all-gather.2.cloned.1.call-update) | async-done | bytes 25165840 | tf_op jit(solution)/shard_map/all_gather | solution.py:16
  208.7 11.5 %fusion.2 = f32[768,256]{1,0:T(8,128)} fusion(f32[768,3072]{1,0:T(8,128)} %param.6, f32[24576,256]{1,0:T(8,128)} %all-gather.2.cloned.1.call-done, s32[]{:T(128)S(6)} %select_n.26), kind=kOutput, calls=%fused_computation.4 | convolution fusion | flops 7247757312 | bytes 13369348 | tf_op jit(solution)/shard_map/dot_general | solution.py:19
  220.2 0.0 reduce-scatter.2.cloned.1.call-update
  220.3 0.0 all-reduce.2.cloned.1.call-start
  220.3 28.0 %reduce-scatter.2.cloned.1.call-done = f32[96,256]{1,0:T(8,128)} async-done(((f32[768,256]{1,0:T(8,128)}), f32[96,256]{1,0:T(8,128)}) %reduce-scatter.2.cloned.1.call-update) | async-done | bytes 98320 | tf_op jit(solution)/shard_map/reduce_scatter | solution.py:18
  248.3 0.0 copy-done
  248.3 0.0 copy-done.5
  248.3 1.2 fusion.14
  249.5 0.0 copy-done.1
  249.5 0.0 copy-start.2
  249.5 1.1 fusion.22
  250.6 0.0 all-reduce.2.cloned.1.call-update
  250.6 256.9 %all-reduce.2.cloned.1.call-done = f32[256,256]{1,0:T(8,128)} async-done(((f32[256,256]{1,0:T(8,128)}), f32[256,256]{1,0:T(8,128)}) %all-reduce.2.cloned.1.call-update) | async-done | bytes 262160 | tf_op jit(solution)/shard_map/psum | solution.py:29
  507.6 0.0 copy-done.3
  507.6 0.0 copy-done.4
  507.6 1.5 convolution_bitcast_fusion
  509.2 2.4 gather_fusion
  511.5 0.4 fusion.5
  511.9 0.6 fusion.23
  512.5 0.1 copy.10
  512.7 2.3 gather_fusion.1
  515.1 0.8 copy.11
  515.9 0.0 copy-done.2
  (2 shorter events, 0.0 us)
Async XLA Ops:
  7.2 241.1 %copy-start = (f32[256,256]{1,0:T(8,128)S(1)}, f32[256,256]{1,0:T(8,128)}, u32[]{:S(2)}) copy-start(f32[256,256]{1,0:T(8,128)} %param.10) | copy-start | bytes 786436
  7.2 242.3 %copy-start.1 = (f32[96,256]{1,0:T(8,128)S(1)}, f32[96,256]{1,0:T(8,128)}, u32[]{:S(2)}) copy-start(f32[96,256]{1,0:T(8,128)} %param.7) | copy-start | bytes 294916
  7.2 241.1 %copy-start.5 = (f32[96,256]{1,0:T(8,128)S(1)}, f32[96,256]{1,0:T(8,128)}, u32[]{:S(2)}) copy-start(f32[96,256]{1,0:T(8,128)} %param.8) | copy-start | bytes 294916
  7.2 500.4 %copy-start.3 = (f32[256,256]{1,0:T(8,128)S(1)}, f32[256,256]{1,0:T(8,128)}, u32[]{:S(2)}) copy-start(f32[256,256]{1,0:T(8,128)} %param.9) | copy-start | bytes 786436
  7.2 500.4 %copy-start.4 = (f32[256,256]{1,0:T(8,128)S(1)}, f32[256,256]{1,0:T(8,128)}, u32[]{:S(2)}) copy-start(f32[256,256]{1,0:T(8,128)} %param.11) | copy-start | bytes 786436
  7.2 201.5 %all-gather.2.cloned.1.call-start = ((), (), s32[]{:S(2)}) async-start(), calls=%async_computation.1 | async-start | bytes 25952256 | tf_op jit(solution)/shard_map/all_gather | solution.py:16
  22.2 226.1 %reduce-scatter.2.cloned.1.call-start = ((), (), s32[]{:S(2)}) async-start(), calls=%async_computation.2 | async-start | bytes 884736 | tf_op jit(solution)/shard_map/reduce_scatter | solution.py:18
  220.3 287.3 %all-reduce.2.cloned.1.call-start = ((), (), s32[]{:S(2)}) async-start(), calls=%async_computation.3 | async-start | bytes 524288 | tf_op jit(solution)/shard_map/psum | solution.py:29
  249.5 266.4 %copy-start.2 = (f32[96,256]{1,0:T(8,128)}, f32[96,256]{1,0:T(8,128)S(1)}, u32[]{:S(2)}) copy-start(f32[96,256]{1,0:T(8,128)S(1)} %fusion.14) | copy-start | bytes 294916
Sparse Core Ops, SparseCore 0:
  22.3 186.4 all-gather.1
  220.4 27.8 reduce-scatter.1
  255.2 252.3 all-reduce.1
where the time goes:
time: 523 us; the launch traced here: 522 us
  waiting for transfers between devices  472 us (90%)
  matrix products  16.3 us (3%)
  blocking collectives  14.9 us (3%)
  between operations  13.9 us (3%)
  local copies, waits for them, and re-layouts  5.71 us (1%)
    psum x1, waiting for transfers between devices, on_device(): gram = lax.psum(local_gram, ('row', 'col'))  257 us
    all_gather x1, waiting for transfers between devices, on_device(): full_panel = lax.all_gather(row_block, 'row', axis=0, tiled=True)  187 us
    reduce_scatter x1, waiting for transfers between devices, on_device(): lax.psum_scatter(jnp.dot(trail_adjoint, column_panel, precision=highest,...  28 us
    all_gather x1, blocking collectives, on_device(): row_block = lax.all_gather(panel, 'col', axis=0, tiled=True)  14.9 us
    dot_general x1, matrix products, on_device(): jnp.dot(trail_adjoint, column_panel, precision=highest, preferred_element...  11.5 us
  transfers between devices with their start and end apart: 3, of which 3 were waited for; matrix products, arithmetic and copies ran while one was open for 0% of the time, Pallas kernels for 0%

commit v1 on v0

--- a/solution.py
+++ b/solution.py
@@ -13,7 +13,8 @@
     col_place = lax.axis_index("col")
     trail_width = trail_adjoint.shape[1]
     row_block = lax.all_gather(panel, "col", axis=0, tiled=True)
-    full_panel = lax.all_gather(row_block, "row", axis=0, tiled=True)
+    repeated = jnp.stack([row_block] * lax.axis_size("row"))
+    full_panel = jnp.concatenate(lax.all_to_all(repeated, "row", 0, 0), axis=0)
     column_panel = lax.dynamic_slice_in_dim(full_panel, col_place * trail_width, trail_width, 0)
     image = lax.psum_scatter(
         jnp.dot(trail_adjoint, column_panel, precision=highest, preferred_element_type=jnp.float32),

time: 523 us -> 955 us (1.83)
  waiting for transfers between devices: 472 us -> 882 us
  starting transfers between devices: 0.12 us -> 11.7 us
  local copies, waits for them, and re-layouts: 5.71 us -> 16.9 us
    all_to_all x0 -> x1, waiting for transfers between devices: none -> 584 us  [on_device(): full_panel = jnp.concatenate(lax.all_to_all(repeated, 'row', 0, 0), axis=0)]
    all_gather x1 -> x0, waiting for transfers between devices: 187 us -> none  [on_device(): full_panel = lax.all_gather(row_block, 'row', axis=0, tiled=True)]
    reduce_scatter x1, waiting for transfers between devices: 28 us -> 40.5 us  [on_device(): lax.psum_scatter(jnp.dot(trail_adjoint, column_panel, precision=highest,...]
    all_to_all x0 -> x1, starting transfers between devices: none -> 11.6 us  [on_device(): full_panel = jnp.concatenate(lax.all_to_all(repeated, 'row', 0, 0), axis=0)]
    another operation x0 -> x1, local copies, waits for them, and re-layouts: none -> 11.1 us  [on_device(): repeated = jnp.stack([row_block] * lax.axis_size('row'))]
where the time goes in v1:
time: 955 us
  waiting for transfers between devices  882 us (92%)
  local copies, waits for them, and re-layouts  16.9 us (2%)
  matrix products  16.3 us (2%)
  between operations  14.2 us (1%)
  blocking collectives  13.9 us (1%)
  starting transfers between devices  11.7 us (1%)
    all_to_all x1, waiting for transfers between devices, on_device(): full_panel = jnp.concatenate(lax.all_to_all(repeated, 'row', 0, 0), axis=0)  584 us
    psum x1, waiting for transfers between devices, on_device(): gram = lax.psum(local_gram, ('row', 'col'))  257 us
    reduce_scatter x1, waiting for transfers between devices, on_device(): lax.psum_scatter(jnp.dot(trail_adjoint, column_panel, precision=highest,...  40.5 us
  transfers between devices with their start and end apart: 3, of which 3 were waited for; matrix products, arithmetic and copies ran while one was open for 0% of the time, Pallas kernels for 0%

profile of v1, /device:TPU:2, one launch (start us, length us, event | category | flops | bytes accessed | tf_op | source)
XLA Modules:
  0.0 954.6 jit_solution(1261486127587217623)
XLA Ops:
  7.2 0.0 copy-start
  7.2 13.9 %all_gather.3 = f32[768,256]{1,0:T(8,128)S(1)} all-gather(f32[96,256]{1,0:T(8,128)} %param.7), channel_id=1, replica_groups=mesh['row'=32,'col'=8] {'col'}, dimensions={0}, use_global_device_ids=true | all-gather | bytes 884736 | tf_op jit(solution)/shard_map/all_gather | solution.py:15
  21.1 11.1 %stack.2 = f32[32,768,256]{2,1,0:T(8,128)} broadcast(f32[768,256]{1,0:T(8,128)S(1)} %all_gather.3), dimensions={1,2} | broadcast | bytes 25952256 | tf_op jit(solution)/shard_map/stack | solution.py:16
  32.2 11.6 %all-to-all-start = ((f32[32,768,256]{2,1,0:T(8,128)}), f32[32,768,256]{2,1,0:T(8,128)}, u32[]{:S(2)}, u32[]{:S(2)}) async-start(f32[32,768,256]{2,1,0:T(8,128)} %stack.2), calls=%async_computation | async-start | bytes 50331648 | tf_op jit(solution)/shard_map/all_to_all | solution.py:17
  43.8 0.0 copy-start.5
  43.8 0.0 copy-start.1
  43.8 0.0 copy-start.3
  43.8 0.0 copy-start.4
  43.8 0.0 reduce-scatter.2.cloned.1.call-start
  43.9 584.2 %all-to-all-done = f32[32,768,256]{2,1,0:T(8,128)} async-done(((f32[32,768,256]{2,1,0:T(8,128)}), f32[32,768,256]{2,1,0:T(8,128)}, u32[]{:S(2)}, u32[]{:S(2)}) %all-to-all-start) | async-done | bytes 25165856 | tf_op jit(solution)/shard_map/all_to_all | solution.py:17
  628.1 11.5 %fusion.2 = f32[768,256]{1,0:T(8,128)} fusion(f32[768,3072]{1,0:T(8,128)} %param.6, f32[24576,256]{1,0:T(8,128)} %bitcast, s32[]{:T(128)S(6)} %select_n.26), kind=kOutput, calls=%fused_computation.4 | convolution fusion | flops 7247757312 | bytes 13369348 | tf_op jit(solution)/shard_map/dot_general | solution.py:20
  639.6 0.0 reduce-scatter.2.cloned.1.call-update
  639.7 0.0 all-reduce.2.cloned.1.call-start
  639.7 40.5 %reduce-scatter.2.cloned.1.call-done = f32[96,256]{1,0:T(8,128)} async-done(((f32[768,256]{1,0:T(8,128)}), f32[96,256]{1,0:T(8,128)}) %reduce-scatter.2.cloned.1.call-update) | async-done | bytes 98320 | tf_op jit(solution)/shard_map/reduce_scatter | solution.py:19
  680.2 0.0 copy-done
  680.2 0.0 copy-done.5
  680.2 1.2 fusion.14
  681.3 0.0 copy-done.1
  681.4 0.0 copy-start.2
  681.4 1.1 fusion.22
  682.5 0.0 all-reduce.2.cloned.1.call-update
  682.5 256.9 %all-reduce.2.cloned.1.call-done = f32[256,256]{1,0:T(8,128)} async-done(((f32[256,256]{1,0:T(8,128)}), f32[256,256]{1,0:T(8,128)}) %all-reduce.2.cloned.1.call-update) | async-done | bytes 262160 | tf_op jit(solution)/shard_map/psum | solution.py:30
  939.4 0.0 copy-done.3
  939.4 0.0 copy-done.4
  939.4 1.5 convolution_bitcast_fusion
  941.0 2.4 gather_fusion
  943.3 0.4 fusion.5
  943.7 0.6 fusion.23
  944.3 0.1 copy.10
  944.5 2.3 gather_fusion.1
  946.9 0.8 copy.11
  947.7 0.0 copy-done.2
  (2 shorter events, 0.0 us)
Async XLA Ops:
  7.2 673.0 %copy-start = (f32[256,256]{1,0:T(8,128)S(1)}, f32[256,256]{1,0:T(8,128)}, u32[]{:S(2)}) copy-start(f32[256,256]{1,0:T(8,128)} %param.10) | copy-start | bytes 786436
  32.2 595.9 %all-to-all-start = ((f32[32,768,256]{2,1,0:T(8,128)}), f32[32,768,256]{2,1,0:T(8,128)}, u32[]{:S(2)}, u32[]{:S(2)}) async-start(f32[32,768,256]{2,1,0:T(8,128)} %stack.2), calls=%async_computation | async-start | bytes 50331648 | tf_op jit(solution)/shard_map/all_to_all | solution.py:17
  43.8 636.4 %copy-start.5 = (f32[96,256]{1,0:T(8,128)S(1)}, f32[96,256]{1,0:T(8,128)}, u32[]{:S(2)}) copy-start(f32[96,256]{1,0:T(8,128)} %param.8) | copy-start | bytes 294916
  43.8 637.5 %copy-start.1 = (f32[96,256]{1,0:T(8,128)S(1)}, f32[96,256]{1,0:T(8,128)}, u32[]{:S(2)}) copy-start(f32[96,256]{1,0:T(8,128)} %param.7) | copy-start | bytes 294916
  43.8 895.6 %copy-start.3 = (f32[256,256]{1,0:T(8,128)S(1)}, f32[256,256]{1,0:T(8,128)}, u32[]{:S(2)}) copy-start(f32[256,256]{1,0:T(8,128)} %param.9) | copy-start | bytes 786436
  43.8 895.6 %copy-start.4 = (f32[256,256]{1,0:T(8,128)S(1)}, f32[256,256]{1,0:T(8,128)}, u32[]{:S(2)}) copy-start(f32[256,256]{1,0:T(8,128)} %param.11) | copy-start | bytes 786436
  43.8 636.3 %reduce-scatter.2.cloned.1.call-start = ((), (), s32[]{:S(2)}) async-start(), calls=%async_computation.2 | async-start | bytes 884736 | tf_op jit(solution)/shard_map/reduce_scatter | solution.py:19
  639.7 299.8 %all-reduce.2.cloned.1.call-start = ((), (), s32[]{:S(2)}) async-start(), calls=%async_computation.3 | async-start | bytes 524288 | tf_op jit(solution)/shard_map/psum | solution.py:30
  681.4 266.4 %copy-start.2 = (f32[96,256]{1,0:T(8,128)}, f32[96,256]{1,0:T(8,128)S(1)}, u32[]{:S(2)}) copy-start(f32[96,256]{1,0:T(8,128)S(1)} %fusion.14) | copy-start | bytes 294916
Sparse Core Ops, SparseCore 0:
  639.8 40.3 reduce-scatter.1
  687.1 252.2 all-reduce.1

commit v2 on v0

--- a/solution.py
+++ b/solution.py
@@ -2,6 +2,11 @@
 import jax.numpy as jnp
 from jax import lax
 from jax.sharding import PartitionSpec as P
+
+
+def remake_rows(content):
+    far_arr = lax.psum(content, axis_name="col")
+    return lax.psum(far_arr, axis_name="row")
 
 
 def lower_half(matrix):
@@ -26,7 +31,7 @@
         updated, diag_inverse, precision=highest, preferred_element_type=jnp.float32
     )
     local_gram = jnp.dot(panel_grad.T, panel, precision=highest, preferred_element_type=jnp.float32)
-    gram = lax.psum(local_gram, ("row", "col"))
+    gram = remake_rows(local_gram)
     corner = diag_adjoint - gram
     inner = lower_half(
         jnp.dot(diag_factor.T, corner, precision=highest, preferred_element_type=jnp.float32)

time: 523 us -> 480 us (0.918)
  waiting for transfers between devices: 472 us -> 429 us
    psum x1 -> x2, waiting for transfers between devices: 257 us -> 214 us  [the longest x1 149 us: remake_rows(): return lax.psum(far_arr, axis_name='row')]
  transfers between devices with their start and end apart: 3 -> 4, of which waited for: 3 -> 4; matrix products, arithmetic and copies ran while one was open for 0% -> 0% of each run, Pallas kernels for 0% -> 0%
where the time goes in v2:
time: 480 us
  waiting for transfers between devices  429 us (89%)
  matrix products  16.3 us (3%)
  blocking collectives  14.9 us (3%)
  between operations  13.9 us (3%)
  local copies, waits for them, and re-layouts  5.71 us (1%)
    all_gather x1, waiting for transfers between devices, on_device(): full_panel = lax.all_gather(row_block, 'row', axis=0, tiled=True)  187 us
    psum x1, waiting for transfers between devices, remake_rows(): return lax.psum(far_arr, axis_name='row')  149 us
    psum x1, waiting for transfers between devices, remake_rows(): far_arr = lax.psum(content, axis_name='col')  65.3 us
    reduce_scatter x1, waiting for transfers between devices, on_device(): lax.psum_scatter(jnp.dot(trail_adjoint, column_panel, precision=highest,...  28 us
    all_gather x1, blocking collectives, on_device(): row_block = lax.all_gather(panel, 'col', axis=0, tiled=True)  14.9 us
    dot_general x1, matrix products, on_device(): jnp.dot(trail_adjoint, column_panel, precision=highest, preferred_element...  11.5 us
  transfers between devices with their start and end apart: 4, of which 4 were waited for; matrix products, arithmetic and copies ran while one was open for 0% of the time, Pallas kernels for 0%

profile of v2, /device:TPU:2, one launch (start us, length us, event | category | flops | bytes accessed | tf_op | source)
XLA Modules:
  0.0 479.7 jit_solution(7794428776500615939)
XLA Ops:
  7.2 0.0 copy-start
  7.2 0.0 copy-start.1
  7.2 0.0 copy-start.5
  7.2 0.0 copy-start.3
  7.2 0.0 copy-start.4
  7.2 0.0 all-gather.2.cloned.1.call-start
  7.3 14.9 %all_gather.6 = f32[768,256]{1,0:T(8,128)} all-gather(f32[96,256]{1,0:T(8,128)} %param.7), channel_id=1, replica_groups=mesh['row'=32,'col'=8] {'col'}, dimensions={0}, use_global_device_ids=true | all-gather | bytes 884736 | tf_op jit(solution)/shard_map/all_gather | solution.py:20
  22.1 0.0 all-gather.2.cloned.1.call-update
  22.2 0.0 reduce-scatter.2.cloned.1.call-start
  22.2 186.5 %all-gather.2.cloned.1.call-done = f32[24576,256]{1,0:T(8,128)} async-done(((f32[768,256]{1,0:T(8,128)}), f32[24576,256]{1,0:T(8,128)}) %all-gather.2.cloned.1.call-update) | async-done | bytes 25165840 | tf_op jit(solution)/shard_map/all_gather | solution.py:21
  208.7 11.5 %fusion.2 = f32[768,256]{1,0:T(8,128)} fusion(f32[768,3072]{1,0:T(8,128)} %param.6, f32[24576,256]{1,0:T(8,128)} %all-gather.2.cloned.1.call-done, s32[]{:T(128)S(6)} %select_n.26), kind=kOutput, calls=%fused_computation.4 | convolution fusion | flops 7247757312 | bytes 13369348 | tf_op jit(solution)/shard_map/dot_general | solution.py:24
  220.2 0.0 reduce-scatter.2.cloned.1.call-update
  220.3 0.0 all-reduce.3.cloned.1.call-start
  220.3 28.0 %reduce-scatter.2.cloned.1.call-done = f32[96,256]{1,0:T(8,128)} async-done(((f32[768,256]{1,0:T(8,128)}), f32[96,256]{1,0:T(8,128)}) %reduce-scatter.2.cloned.1.call-update) | async-done | bytes 98320 | tf_op jit(solution)/shard_map/reduce_scatter | solution.py:23
  248.3 0.0 copy-done
  248.3 0.0 copy-done.5
  248.3 1.2 fusion.14
  249.5 0.0 copy-done.1
  249.5 0.0 copy-start.2
  249.5 1.1 fusion.22
  250.6 0.0 all-reduce.3.cloned.1.call-update
  250.6 0.0 all-reduce.5.cloned.1.call-start
  250.7 65.3 %all-reduce.3.cloned.1.call-done = f32[256,256]{1,0:T(8,128)} async-done(((f32[256,256]{1,0:T(8,128)}), f32[256,256]{1,0:T(8,128)}) %all-reduce.3.cloned.1.call-update) | async-done | bytes 262160 | tf_op jit(solution)/shard_map/psum | solution.py:8
  316.0 0.0 all-reduce.5.cloned.1.call-update
  316.0 148.8 %all-reduce.5.cloned.1.call-done = f32[256,256]{1,0:T(8,128)} async-done(((f32[256,256]{1,0:T(8,128)}), f32[256,256]{1,0:T(8,128)}) %all-reduce.5.cloned.1.call-update) | async-done | bytes 262160 | tf_op jit(solution)/shard_map/psum | solution.py:9
  464.9 0.0 copy-done.3
  464.9 0.0 copy-done.4
  464.9 1.5 convolution_bitcast_fusion
  466.4 2.4 gather_fusion
  468.8 0.4 fusion.5
  469.2 0.6 fusion.23
  469.8 0.1 copy.10
  469.9 2.3 gather_fusion.1
  472.3 0.8 copy.11
  473.2 0.0 copy-done.2
  (2 shorter events, 0.0 us)
Async XLA Ops:
  7.2 241.1 %copy-start = (f32[256,256]{1,0:T(8,128)S(1)}, f32[256,256]{1,0:T(8,128)}, u32[]{:S(2)}) copy-start(f32[256,256]{1,0:T(8,128)} %param.10) | copy-start | bytes 786436
  7.2 242.3 %copy-start.1 = (f32[96,256]{1,0:T(8,128)S(1)}, f32[96,256]{1,0:T(8,128)}, u32[]{:S(2)}) copy-start(f32[96,256]{1,0:T(8,128)} %param.7) | copy-start | bytes 294916
  7.2 241.1 %copy-start.5 = (f32[96,256]{1,0:T(8,128)S(1)}, f32[96,256]{1,0:T(8,128)}, u32[]{:S(2)}) copy-start(f32[96,256]{1,0:T(8,128)} %param.8) | copy-start | bytes 294916
  7.2 457.7 %copy-start.3 = (f32[256,256]{1,0:T(8,128)S(1)}, f32[256,256]{1,0:T(8,128)}, u32[]{:S(2)}) copy-start(f32[256,256]{1,0:T(8,128)} %param.9) | copy-start | bytes 786436
  7.2 457.6 %copy-start.4 = (f32[256,256]{1,0:T(8,128)S(1)}, f32[256,256]{1,0:T(8,128)}, u32[]{:S(2)}) copy-start(f32[256,256]{1,0:T(8,128)} %param.11) | copy-start | bytes 786436
  7.2 201.5 %all-gather.2.cloned.1.call-start = ((), (), s32[]{:S(2)}) async-start(), calls=%async_computation.1 | async-start | bytes 25952256 | tf_op jit(solution)/shard_map/all_gather | solution.py:21
  22.2 226.1 %reduce-scatter.2.cloned.1.call-start = ((), (), s32[]{:S(2)}) async-start(), calls=%async_computation.2 | async-start | bytes 884736 | tf_op jit(solution)/shard_map/reduce_scatter | solution.py:23
  220.3 95.8 %all-reduce.3.cloned.1.call-start = ((), (), s32[]{:S(2)}) async-start(), calls=%async_computation.3 | async-start | bytes 524288 | tf_op jit(solution)/shard_map/psum | solution.py:8
  249.5 223.7 %copy-start.2 = (f32[96,256]{1,0:T(8,128)}, f32[96,256]{1,0:T(8,128)S(1)}, u32[]{:S(2)}) copy-start(f32[96,256]{1,0:T(8,128)S(1)} %fusion.14) | copy-start | bytes 294916
  250.6 214.2 %all-reduce.5.cloned.1.call-start = ((), (), s32[]{:S(2)}) async-start(), calls=%async_computation.4 | async-start | bytes 524288 | tf_op jit(solution)/shard_map/psum | solution.py:9
Sparse Core Ops, SparseCore 0:
  22.3 186.4 all-gather.1
  220.4 27.8 reduce-scatter.1
  251.3 64.6 all-reduce.2
  319.3 145.4 all-reduce.4
